TPU v7x, 256 devices: a whole 4x4x8 slice. The times are simulated.
256 devices in a mesh: inner: 8 (over x, core), outer: 32 (over z, y).
Axes of the slice: x: 4, y: 4, z: 8, core: 2. Of those that a mesh axis runs over, the one named last changes fastest.
Arguments:
- queries: bfloat16 [32768, 2048], P(('outer', 'inner')), may hold values from -6 to 6
- keys: bfloat16 [32768, 2048], P(('outer', 'inner')), may hold values from -6 to 6
- values: bfloat16 [32768, 2048], P(('outer', 'inner')), may hold values from -6 to 6
- out_grad: bfloat16 [32768, 2048], P(('outer', 'inner')), may hold values from -6 to 6
- positions: int32 [32768], P(('outer', 'inner')), may hold values from 0 to 8191
Outputs:
- attended: bfloat16 [32768, 2048], P(('outer', 'inner'))
- query_grad: bfloat16 [32768, 2048], P(('outer', 'inner'))
- key_grad: bfloat16 [32768, 2048], P(('outer', 'inner'))
- value_gradient: bfloat16 [32768, 2048], P(('outer', 'inner'))
All inputs are finite; a program needn't handle non-finite values.
Results may differ from a plain program's by a relative error of at most 0.0064.
Values sent between devices are 32-bit elements; how exact they have to be, the bound alone decides.
A program may use at most 256 MiB of HBM per device.

v0:
```python
import math

import jax
import jax.numpy as jnp
from jax import lax
from jax.sharding import PartitionSpec as P

D_HEAD = 128


def carried_in(value, axis, join, neutral, backward):
    count, mine = (lax.axis_size(axis), lax.axis_index(axis))
    pieces = lax.all_gather(value, axis)
    if backward:
        pieces = pieces[::-1]
        mine = count - 1 - mine
    so_far = jnp.full_like(value, 0) + jnp.asarray(neutral, value.dtype)

    def step(position, so_far):
        longer = join(so_far, pieces[position])
        return jnp.where(position < mine, longer, so_far)

    return lax.fori_loop(0, count - 1, step, so_far)


def rotary_tables(positions, head_dim):
    half_dim = head_dim // 2
    spacing = jnp.arange(half_dim).astype(jnp.float32) * (-2.0 * math.log(500000.0) / head_dim)
    angle = positions.astype(jnp.float32)[:, None] * jnp.exp(spacing)[None, :]
    return (jnp.cos(angle)[:, None, :], jnp.sin(angle)[:, None, :])


def rotate(rows, cosine, sine):
    half_dim = rows.shape[-1] // 2
    first = rows[..., :half_dim].astype(jnp.float32)
    second = rows[..., half_dim:].astype(jnp.float32)
    return jnp.concatenate(
        [first * cosine - second * sine, second * cosine + first * sine], axis=-1
    )


def unrotate(rows, cosine, sine):
    half_dim = rows.shape[-1] // 2
    first = rows[..., :half_dim]
    second = rows[..., half_dim:]
    return jnp.concatenate(
        [first * cosine + second * sine, second * cosine - first * sine], axis=-1
    )


def add_states(earlier, later):
    return earlier + later


def outer_sums(keys_group, queries_group):
    zero_part = jnp.zeros_like(keys_group)
    keys_earlier = carried_in(keys_group, "outer", add_states, zero_part, False)
    queries_later = carried_in(queries_group, "outer", add_states, zero_part, True)
    return (keys_earlier, queries_later)


def shards(queries, keys, values, out_grad, positions):
    rows_here = queries.shape[0]
    head_dim = D_HEAD
    heads_count = queries.shape[1] // head_dim
    total_tokens = rows_here * lax.axis_size("inner") * lax.axis_size("outer")
    scale_factor = (head_dim * total_tokens) ** (-0.5)
    cosine, sine = rotary_tables(positions, head_dim)
    shaped = (rows_here, heads_count, head_dim)
    rotated_query = rotate(queries.reshape(shaped), cosine, sine).astype(jnp.bfloat16)
    rotated_key = rotate(keys.reshape(shaped), cosine, sine).astype(jnp.bfloat16)
    value_row_block = values.reshape(shaped)
    gradient_row_block = out_grad.reshape(shaped)
    key_value_state = jnp.einsum(
        "pob,poj->obj", rotated_key, value_row_block, preferred_element_type=jnp.float32
    )
    query_state = jnp.einsum(
        "pob,poj->obj", rotated_query, gradient_row_block, preferred_element_type=jnp.float32
    )
    own_place = lax.axis_index("inner")
    piece = (
        lax.all_gather(key_value_state[None], "inner", axis=0, tiled=True),
        lax.all_gather(query_state[None], "inner", axis=0, tiled=True),
    )
    count = piece[0].shape[0]
    order = jnp.arange(count, dtype=jnp.int32)
    earlier = (order < own_place)[:, None, None, None]
    later = (order > own_place)[:, None, None, None]
    keys_before = jnp.sum(jnp.where(earlier, piece[0], 0.0), axis=0)
    queries_after = jnp.sum(jnp.where(later, piece[1], 0.0), axis=0)
    keys_group = jnp.sum(piece[0], axis=0)
    queries_group = jnp.sum(piece[1], axis=0)
    keys_earlier, queries_later = outer_sums(keys_group, queries_group)
    preceding_state = (keys_earlier + keys_before).astype(jnp.bfloat16)
    following_state = (queries_later + queries_after).astype(jnp.bfloat16)
    causal = (jnp.arange(rows_here)[:, None] >= jnp.arange(rows_here)[None, :])[None]
    score_matrix = jnp.where(
        causal,
        jnp.einsum("thd,shd->hts", rotated_query, rotated_key, preferred_element_type=jnp.float32),
        0.0,
    ).astype(jnp.bfloat16)
    score_gradient = jnp.where(
        causal,
        jnp.einsum(
            "thd,shd->hts", gradient_row_block, value_row_block, preferred_element_type=jnp.float32
        ),
        0.0,
    ).astype(jnp.bfloat16)
    attended = scale_factor * (
        jnp.einsum(
            "rgb,brf->grf", score_matrix, value_row_block, preferred_element_type=jnp.float32
        )
        + jnp.einsum(
            "axz,xzo->axo", rotated_query, preceding_state, preferred_element_type=jnp.float32
        )
    )
    rotated_query_gradient = scale_factor * (
        jnp.einsum("rgb,brf->grf", score_gradient, rotated_key, preferred_element_type=jnp.float32)
        + jnp.einsum(
            "xge,gme->xgm", gradient_row_block, preceding_state, preferred_element_type=jnp.float32
        )
    )
    rotated_key_gradient = scale_factor * (
        jnp.einsum(
            "uox,oul->xul", score_gradient, rotated_query, preferred_element_type=jnp.float32
        )
        + jnp.einsum(
            "olb,lfb->olf", value_row_block, following_state, preferred_element_type=jnp.float32
        )
    )
    value_gradient = scale_factor * (
        jnp.einsum(
            "uox,oul->xul", score_matrix, gradient_row_block, preferred_element_type=jnp.float32
        )
        + jnp.einsum(
            "tyg,yge->tye", rotated_key, following_state, preferred_element_type=jnp.float32
        )
    )
    flat = (rows_here, heads_count * head_dim)
    return (
        attended.astype(jnp.bfloat16).reshape(flat),
        unrotate(rotated_query_gradient, cosine, sine).astype(jnp.bfloat16).reshape(flat),
        unrotate(rotated_key_gradient, cosine, sine).astype(jnp.bfloat16).reshape(flat),
        value_gradient.astype(jnp.bfloat16).reshape(flat),
    )


def solution(mesh):
    placed = (
        P(("outer", "inner"), None),
        P(("outer", "inner"), None),
        P(("outer", "inner"), None),
        P(("outer", "inner"), None),
        P(("outer", "inner")),
    )
    return jax.shard_map(
        shards,
        mesh=mesh,
        in_specs=placed,
        out_specs=(
            P(("outer", "inner"), None),
            P(("outer", "inner"), None),
            P(("outer", "inner"), None),
            P(("outer", "inner"), None),
        ),
        check_vma=False,
    )
```

profile of v0, /device:TPU:1, one launch (start us, length us, event | category | flops | bytes accessed | tf_op | source)
XLA Modules:
  0.0 743.1 jit_solution(15101625095384080709)
XLA Ops:
  13.8 56.5 %all-gather.13.cloned.1.call-done = f32[128,128,128]{2,1,0:T(8,128)} async-done(((f32[16,128,128]{2,1,0:T(8,128)}), f32[128,128,128]{2,1,0:T(8,128)}) %all-gather.13.cloned.1.call-update) | async-done | bytes 8388624 | tf_op jit(solution)/shard_map/all_gather | solution.py:83
  70.3 6.1 select_reduce_fusion
  78.6 2.0 copy.101
  83.4 225.2 %all-gather.15.cloned.1.call-done = f32[512,128,128]{2,1,0:T(8,128)} async-done(((f32[16,128,128]{2,1,0:T(8,128)}), f32[512,128,128]{2,1,0:T(8,128)}) %all-gather.15.cloned.1.call-update) | async-done | bytes 33554448 | tf_op jit(solution)/shard_map/all_gather | solution.py:13
  308.6 23.0 %rev.3 = f32[32,16,128,128]{3,2,1,0:T(8,128)} reverse(f32[32,16,128,128]{3,2,1,0:T(8,128)} %bitcast.85), dimensions={0} | reverse | bytes 67108864 | tf_op jit(solution)/shard_map/rev | solution.py:15
  331.6 50.0 %while.29 = (s32[]{:T(128)}, f32[16,128,128]{2,1,0:T(8,128)S(1)}, s32[]{:T(128)}, f32[32,16,128,128]{3,2,1,0:T(8,128)}, s32[]{:T(128)}, /*index=5*/s32[]{:T(128)}) while((s32[]{:T(128)}, f32[16,128,128]{2,1,0:T(8,128)S(1)}, s32[]{:T(128)}, f32[32,16,128,128]{3,2,1,0:T(8,128)}, s32[]{:T(128)}, /*index=5*/s32[]{:T(128)}) %tuple.77), condition=%wide.region_6.7_spmd.clone, body=%wide.region_5.6_spmd.clone.sunk | while | flops 786436 | bytes 3145821 | solution.py:23
  333.2 1.6 add_select_fusion.5
  334.8 1.6 add_select_fusion.5
  339.7 1.6 add_select_fusion.5
  341.3 1.6 add_select_fusion.5
  342.9 1.6 add_select_fusion.5
  383.0 1.9 fusion.5
  384.9 2.6 add_convert_fusion
  389.5 50.3 %all-gather.9.cloned.1.call-done = f32[128,128,128]{2,1,0:T(8,128)} async-done(((f32[16,128,128]{2,1,0:T(8,128)}), f32[128,128,128]{2,1,0:T(8,128)}) %all-gather.9.cloned.1.call-update) | async-done | bytes 8388624 | tf_op jit(solution)/shard_map/all_gather | solution.py:82
  439.8 6.1 select_reduce_fusion.1
  446.4 1.7 convolution_bitcast_fusion.1
  449.3 2.0 copy.88
  451.3 2.3 pad_maximum_fusion.3
  453.6 2.0 copy.82
  455.7 2.0 copy.87
  457.7 2.6 convolution_bitcast_fusion.3
  460.3 217.8 %all-gather.11.cloned.1.call-done = f32[512,128,128]{2,1,0:T(8,128)} async-done(((f32[16,128,128]{2,1,0:T(8,128)}), f32[512,128,128]{2,1,0:T(8,128)}) %all-gather.11.cloned.1.call-update) | async-done | bytes 33554448 | tf_op jit(solution)/shard_map/all_gather | solution.py:13
  678.1 50.0 %while.28 = (s32[]{:T(128)}, f32[16,128,128]{2,1,0:T(8,128)S(1)}, s32[]{:T(128)}, f32[32,16,128,128]{3,2,1,0:T(8,128)}, s32[]{:T(128)}, /*index=5*/s32[]{:T(128)}) while((s32[]{:T(128)}, f32[16,128,128]{2,1,0:T(8,128)S(1)}, s32[]{:T(128)}, f32[32,16,128,128]{3,2,1,0:T(8,128)}, s32[]{:T(128)}, /*index=5*/s32[]{:T(128)}) %tuple.91), condition=%wide.region_2.3_spmd.clone, body=%wide.region_1.2_spmd.clone.sunk | while | flops 786436 | bytes 3145821 | solution.py:23
  733.7 1.9 fusion.8
  (109 shorter events, 113.6 us)
Async XLA Ops:
  7.2 74.4 %copy-start = (bf16[128,2048]{1,0:T(8,128)(2,1)S(1)}, bf16[128,2048]{1,0:T(8,128)(2,1)}, u32[]{:S(2)}) copy-start(bf16[128,2048]{1,0:T(8,128)(2,1)} %param.11) | copy-start | bytes 1572868
  7.2 63.1 %all-gather.13.cloned.1.call-start = ((), (), s32[]{:S(2)}) async-start(), calls=%async_computation.2 | async-start | bytes 9437184 | tf_op jit(solution)/shard_map/all_gather | solution.py:83
  13.8 294.8 %all-gather.15.cloned.1.call-start = ((), (), s32[]{:S(2)}) async-start(), calls=%async_computation.3 | async-start | bytes 34603008 | tf_op jit(solution)/shard_map/all_gather | solution.py:13
  76.4 363.4 %all-gather.9.cloned.1.call-start = ((), (), s32[]{:S(2)}) async-start(), calls=%async_computation | async-start | bytes 9437184 | tf_op jit(solution)/shard_map/all_gather | solution.py:82
  82.1 249.5 %copy-start.4 = (bf16[16,128,128]{2,1,0:T(8,128)(2,1)}, bf16[16,128,128]{2,1,0:T(8,128)(2,1)S(1)}, u32[]{:S(2)}) copy-start(bf16[16,128,128]{2,1,0:T(8,128)(2,1)S(1)} %fusion.11) | copy-start | bytes 1572868
  383.0 62.9 %copy-start.3 = (bf16[16,128,128]{2,1,0:T(8,128)(2,1)}, bf16[16,128,128]{2,1,0:T(8,128)(2,1)S(1)}, u32[]{:S(2)}) copy-start(bf16[16,128,128]{2,1,0:T(8,128)(2,1)S(1)} %add_convert_fusion.1) | copy-start | bytes 1572868
  389.2 288.8 %all-gather.11.cloned.1.call-start = ((), (), s32[]{:S(2)}) async-start(), calls=%async_computation.1 | async-start | bytes 34603008 | tf_op jit(solution)/shard_map/all_gather | solution.py:13
  446.4 1.8 copy-start.2
  729.5 0.8 copy-start.1
Sparse Core Ops, SparseCore 0:
  13.9 56.3 all-gather.12
  76.6 232.0 all-gather.14
  389.4 50.3 all-gather.8
  446.0 232.0 all-gather.10
where the time goes:
time: 746 us; the launch traced here: 743 us
  waiting for transfers between devices  550 us (74%)
  other arithmetic  121 us (16%)
  local copies, waits for them, and re-layouts  40 us (5%)
  matrix products  16.5 us (2%)
  between operations  14 us (2%)
    all_gather x2, waiting for transfers between devices, carried_in(): pieces = lax.all_gather(value, axis)  443 us
    select_n x62, other arithmetic, step(): return jnp.where(position < mine, longer, so_far)  98.5 us
    all_gather x1, waiting for transfers between devices, shards(): lax.all_gather(query_state[None], 'inner', axis=0, tiled=True)  56.5 us
    all_gather x1, waiting for transfers between devices, shards(): lax.all_gather(key_value_state[None], 'inner', axis=0, tiled=True)  50.3 us
    rev x1, local copies, waits for them, and re-layouts, carried_in(): pieces = pieces[::-1]  23 us
  transfers between devices with their start and end apart: 4, of which 4 were waited for; matrix products, arithmetic and copies ran while one was open for 3% of the time, Pallas kernels for 0%

commit v1 on v0

v1 whole, which is shorter than its diff:
```python
import functools
import math

import jax
import jax.numpy as jnp
from jax import lax
from jax.experimental import pallas as pl
from jax.experimental.pallas import tpu as pltpu
from jax.sharding import PartitionSpec as P

D_HEAD = 128
CORES = 2
F32, BF16 = (jnp.float32, jnp.bfloat16)


def rotate(rows, cosine, sine):
    rows = rows.astype(F32)
    return rows * cosine + pltpu.roll(rows, D_HEAD // 2, 1) * sine


def unrotate(rows, cosine, sine):
    return rows * cosine - pltpu.roll(rows, D_HEAD // 2, 1) * sine


def dot(left, right, left_dim, right_dim):
    return lax.dot_general(
        left, right, (((left_dim,), (right_dim,)), ((), ())), preferred_element_type=F32
    )


def columns(head):
    return pl.ds(pl.multiple_of(head * D_HEAD, D_HEAD), D_HEAD)


def scan_kernel(
    sizes,
    q_ref, k_ref, v_ref, g_ref, cos_ref, sin_ref,
    before_ref, after_ref,
    theirs, own, pin, chip, xin, row, yin, plane, zin, yout, ybase, xout, xbase, pout, pbase,
    core_s, core_r, x_s, x_r, y_s, y_r, z_s, z_r, yb_s, yb_r, xb_s, xb_r, cb_s, cb_r,
):
    nx, ny, nz, per = sizes
    inner, outer = (lax.axis_index("inner"), lax.axis_index("outer"))
    x, c = (inner // CORES, lax.rem(inner, CORES))
    z, y = (outer // ny, lax.rem(outer, ny))
    part = D_HEAD // ny
    other = 1 - c

    def at(xx, cc, yy, zz):
        return {"inner": xx * CORES + cc, "outer": zz * ny + yy}

    def shifted(place, by, count):
        return lax.rem(place + by, count)

    partner = at(x, other, y, z)
    x_dev = [at(shifted(x, d, nx), c, y, z) for d in range(nx)]
    y_dev = [at(x, c, shifted(y, d, ny), z) for d in range(ny)]
    z_dev = [at(x, c, y, shifted(z, d, nz)) for d in range(nz)]
    barrier = pltpu.get_barrier_semaphore()
    peers = [partner] + x_dev[1:] + y_dev[1:] + z_dev[1:]
    for peer in peers:
        pl.semaphore_signal(barrier, inc=1, device_id=peer, device_id_type=pl.DeviceIdType.MESH)

    sent = []

    def remote(src, dst, send, recv, device):
        return pltpu.make_async_remote_copy(
            src_ref=src, dst_ref=dst, send_sem=send, recv_sem=recv,
            device_id=device, device_id_type=pl.DeviceIdType.MESH,
        )

    def post(*args):
        copy = remote(*args)
        copy.start()
        sent.append(copy)

    cosine, sine = (cos_ref[...], sin_ref[...])
    far_first = sorted(range(nx), key=lambda d: (d == 0, -min(d, nx - d)))

    def states(head, put):
        at_head = columns(head)
        key = rotate(k_ref[:, at_head], cosine, sine).astype(BF16)
        put[0] = dot(key, v_ref[:, at_head], 0, 0)
        query = rotate(q_ref[:, at_head], cosine, sine).astype(BF16)
        put[1] = dot(query, g_ref[:, at_head], 0, 0)

    def head_of(xx, cc, j):
        return (xx * CORES + cc) * per + j

    first = True
    for j in range(per):
        for d in far_first:
            xx = shifted(x, d, nx)
            states(head_of(xx, other, j), theirs.at[xx, j])
            if first:
                pl.semaphore_wait(barrier, len(peers))
                first = False
            post(theirs.at[xx, j], pin.at[xx, j], core_s.at[d, j], core_r.at[d, j], partner)
    for j in range(per):
        for d in far_first:
            xx = shifted(x, d, nx)
            states(head_of(xx, c, j), own.at[xx, j])

    for j in range(per):
        for d in far_first:
            xx = shifted(x, d, nx)
            remote(theirs.at[xx, j], pin.at[xx, j], core_s.at[d, j], core_r.at[d, j], partner).wait_recv()
            if d:
                chip[xx, j] = own[xx, j] + pin[xx, j]
                post(chip.at[xx, j], xin.at[x, j], x_s.at[d, j], x_r.at[d, j], x_dev[d])
            else:
                xin[x, j] = own[x, j] + pin[x, j]

    for j in range(per):
        for d in range(1, nx):
            src = shifted(x, nx - d, nx)
            remote(chip.at[src, j], xin.at[src, j], x_s.at[d, j], x_r.at[d, j], x_dev[d]).wait_recv()
        total = xin[0, j]
        for xx in range(1, nx):
            total = total + xin[xx, j]
        row[j] = total
        for d in range(1, ny):
            rows = pl.ds(pl.multiple_of(shifted(y, d, ny) * part, part), part)
            post(row.at[j, :, rows], yin.at[y, j], y_s.at[d, j], y_r.at[d, j], y_dev[d])
        yin[y, j] = row[j, :, pl.ds(pl.multiple_of(y * part, part), part)]

    for j in range(per):
        for d in range(1, ny):
            src = shifted(y, ny - d, ny)
            remote(yout.at[src, j], yin.at[src, j], y_s.at[d, j], y_r.at[d, j], y_dev[d]).wait_recv()
        total = yin[0, j]
        for yy in range(1, ny):
            total = total + yin[yy, j]
        plane[j] = total
        for d in range(1, nz):
            which = jnp.where(z + d >= nz, 1, 0)
            post(plane.at[j, which], zin.at[z, j], z_s.at[d, j], z_r.at[d, j], z_dev[d])
        zin[z, j] = jnp.zeros((part, D_HEAD), F32)

    for j in range(per):
        for d in range(1, nz):
            src = shifted(z, nz - d, nz)
            remote(plane.at[j, 0], zin.at[src, j], z_s.at[d, j], z_r.at[d, j], z_dev[d]).wait_recv()
        earlier = jnp.zeros((part, D_HEAD), F32)
        later = jnp.zeros((part, D_HEAD), F32)
        for zz in range(nz):
            piece = zin[zz, j]
            earlier = earlier + jnp.where(zz < z, piece, 0.0)
            later = later + jnp.where(zz > z, piece, 0.0)
        for yy in range(ny):
            yout[yy, j, 0] = earlier
            earlier = earlier + yin[yy, j, 0]
        for yy in reversed(range(ny)):
            yout[yy, j, 1] = later
            later = later + yin[yy, j, 1]
        mine = pl.ds(pl.multiple_of(y * part, part), part)
        for d in range(1, ny):
            yy = shifted(y, d, ny)
            post(yout.at[yy, j], ybase.at[j, :, mine], yb_s.at[d, j], yb_r.at[d, j], y_dev[d])
        ybase[j, :, mine] = yout[y, j]

    for j in range(per):
        for d in range(1, ny):
            src = shifted(y, ny - d, ny)
            rows = pl.ds(pl.multiple_of(src * part, part), part)
            remote(yout.at[src, j], ybase.at[j, :, rows], yb_s.at[d, j], yb_r.at[d, j], y_dev[d]).wait_recv()
        earlier = ybase[j, 0]
        for xx in range(nx):
            xout[xx, j, 0] = earlier
            earlier = earlier + xin[xx, j, 0]
        later = ybase[j, 1]
        for xx in reversed(range(nx)):
            xout[xx, j, 1] = later
            later = later + xin[xx, j, 1]
        for d in far_first:
            xx = shifted(x, d, nx)
            if d:
                post(xout.at[xx, j], xbase.at[x, j], xb_s.at[d, j], xb_r.at[d, j], x_dev[d])
            else:
                xbase[x, j] = xout[x, j]

    for j in range(per):
        for d in reversed(far_first):
            src = shifted(x, nx - d, nx)
            if d:
                remote(xout.at[src, j], xbase.at[src, j], xb_s.at[d, j], xb_r.at[d, j], x_dev[d]).wait_recv()
            keys, queries = (xbase[src, j, 0], xbase[src, j, 1])
            pout[src, j, 0] = keys + jnp.where(c == 0, own[src, j, 0], 0.0)
            pout[src, j, 1] = queries + jnp.where(c == 1, own[src, j, 1], 0.0)
            post(pout.at[src, j], pbase.at[src, j], cb_s.at[d, j], cb_r.at[d, j], partner)
            head = head_of(src, c, j)
            before_ref[head] = (keys + jnp.where(c == 1, pin[src, j, 0], 0.0)).astype(BF16)
            after_ref[head] = (queries + jnp.where(c == 0, pin[src, j, 1], 0.0)).astype(BF16)

    for j in range(per):
        for d in reversed(far_first):
            src = shifted(x, nx - d, nx)
            remote(pout.at[src, j], pbase.at[src, j], cb_s.at[d, j], cb_r.at[d, j], partner).wait_recv()
            head = head_of(src, other, j)
            before_ref[head] = pbase[src, j, 0].astype(BF16)
            after_ref[head] = pbase[src, j, 1].astype(BF16)
    for copy in sent:
        copy.wait_send()


def block_kernel(
    scale, heads, q_ref, k_ref, v_ref, g_ref, cos_ref, sin_ref, before_ref, after_ref,
    attended_ref, query_grad_ref, key_grad_ref, value_grad_ref,
):
    cosine, sine = (cos_ref[...], sin_ref[...])
    tokens = q_ref.shape[0]
    causal = lax.broadcasted_iota(jnp.int32, (tokens, tokens), 0) >= lax.broadcasted_iota(
        jnp.int32, (tokens, tokens), 1
    )
    for n in range(heads):
        cols = slice(n * D_HEAD, (n + 1) * D_HEAD)
        query = rotate(q_ref[:, cols], cosine, sine).astype(BF16)
        key = rotate(k_ref[:, cols], cosine, sine).astype(BF16)
        value, grad = (v_ref[:, cols], g_ref[:, cols])
        before, after = (before_ref[n], after_ref[n])
        scores = jnp.where(causal, dot(query, key, 1, 1), 0.0).astype(BF16)
        grad_scores = jnp.where(causal, dot(grad, value, 1, 1), 0.0).astype(BF16)
        attended = dot(scores, value, 1, 0) + dot(query, before, 1, 0)
        attended_ref[:, cols] = (scale * attended).astype(BF16)
        query_grad = scale * (dot(grad_scores, key, 1, 0) + dot(grad, before, 1, 1))
        query_grad_ref[:, cols] = unrotate(query_grad, cosine, sine).astype(BF16)
        key_grad = scale * (dot(grad_scores, query, 0, 0) + dot(value, after, 1, 1))
        key_grad_ref[:, cols] = unrotate(key_grad, cosine, sine).astype(BF16)
        value_grad = scale * (dot(scores, grad, 0, 0) + dot(key, after, 1, 0))
        value_grad_ref[:, cols] = value_grad.astype(BF16)


def shards(sizes, queries, keys, values, out_grad, positions):
    nx, ny, nz, per = sizes
    tokens, width = queries.shape
    heads = width // D_HEAD
    total_tokens = tokens * lax.axis_size("inner") * lax.axis_size("outer")
    scale = (D_HEAD * total_tokens) ** (-0.5)
    half = D_HEAD // 2
    spacing = jnp.arange(half).astype(F32) * (-2.0 * math.log(500000.0) / D_HEAD)
    angle = positions.astype(F32)[:, None] * jnp.exp(spacing)[None, :]
    cosine, sine = (jnp.cos(angle), jnp.sin(angle))
    cosine = jnp.concatenate([cosine, cosine], axis=1)
    sine = jnp.concatenate([-sine, sine], axis=1)

    part = D_HEAD // ny
    square = (per, 2, D_HEAD, D_HEAD)
    by_x = pltpu.VMEM((nx,) + square, F32)
    by_y = pltpu.VMEM((ny, per, 2, part, D_HEAD), F32)
    whole = pl.BlockSpec(memory_space=pltpu.VMEM)
    sems = []
    for count in (nx, nx, ny, nz, ny, nx, nx):
        sems += [pltpu.SemaphoreType.DMA((count, per))] * 2
    before, after = pl.pallas_call(
        functools.partial(scan_kernel, sizes),
        out_shape=[jax.ShapeDtypeStruct((heads, D_HEAD, D_HEAD), BF16)] * 2,
        in_specs=[whole] * 6,
        out_specs=[whole] * 2,
        scratch_shapes=[
            by_x, by_x, by_x, by_x, by_x,
            pltpu.VMEM(square, F32),
            by_y,
            pltpu.VMEM((per, 2, part, D_HEAD), F32),
            pltpu.VMEM((nz, per, part, D_HEAD), F32),
            by_y,
            pltpu.VMEM(square, F32),
            by_x, by_x, by_x, by_x,
        ] + sems,
        compiler_params=pltpu.CompilerParams(
            collective_id=0, has_side_effects=True, vmem_limit_bytes=48 * 1024 * 1024
        ),
        name="scan",
    )(queries, keys, values, out_grad, cosine, sine)

    at_once = 4
    rows = pl.BlockSpec((tokens, at_once * D_HEAD), lambda n: (0, n))
    table = pl.BlockSpec((tokens, D_HEAD), lambda n: (0, 0))
    state = pl.BlockSpec((at_once, D_HEAD, D_HEAD), lambda n: (n, 0, 0))
    return pl.pallas_call(
        functools.partial(block_kernel, scale, at_once),
        grid=(heads // at_once,),
        out_shape=[jax.ShapeDtypeStruct((tokens, width), BF16)] * 4,
        in_specs=[rows] * 4 + [table] * 2 + [state] * 2,
        out_specs=[rows] * 4,
        name="block",
    )(queries, keys, values, out_grad, cosine, sine, before, after)


def solution(mesh):
    inner, outer = (mesh.shape["inner"], mesh.shape["outer"])
    ny = 4 if outer % 16 == 0 else 2
    sizes = (inner // CORES, ny, outer // ny, 16 // inner)
    both = P(("outer", "inner"), None)
    return jax.shard_map(
        functools.partial(shards, sizes),
        mesh=mesh,
        in_specs=(both,) * 4 + (P(("outer", "inner")),),
        out_specs=(both,) * 4,
        check_vma=False,
    )
```

time: 746 us -> 63.3 us (0.08)
  waiting for transfers between devices: 550 us -> 0 us
  other arithmetic: 121 us -> 1.14 us
  Pallas kernels: 0 us -> 56.4 us
  local copies, waits for them, and re-layouts: 40 us -> 4.73 us
  matrix products: 16.5 us -> 0 us
  between operations: 14 us -> 0.72 us
    all_gather x4 -> x0, waiting for transfers between devices: 550 us -> none  [the longest x2 443 us: carried_in(): pieces = lax.all_gather(value, axis)]
    select_n x62 -> x0, other arithmetic: 98.5 us -> none  [step(): return jnp.where(position < mine, longer, so_far)]
    pallas_call x0 -> x2, Pallas kernels: none -> 56.4 us  [the longest x1 49.6 us: shards(): pl.pallas_call(functools.partial(scan_kernel, sizes), out_shape=[jax.Shap...]
    rev x1 -> x0, local copies, waits for them, and re-layouts: 23 us -> none  [carried_in(): pieces = pieces[::-1]]
    dot_general x12 -> x0, matrix products: 16.5 us -> none  [the longest x1 2.61 us: shards(): jnp.einsum('rgb,brf->grf', score_matrix, value_row_block, preferred_eleme...]
    reduce_sum x2 -> x0, other arithmetic: 12.2 us -> none  [the longest x1 6.1 us: shards(): keys_before = jnp.sum(jnp.where(earlier, piece[0], 0.0), axis=0)]
    unnamed x20 -> x16, local copies, waits for them, and re-layouts: 12.6 us -> 4.73 us
  transfers between devices with their start and end apart: 4 -> 0, of which waited for: 4 -> 0; matrix products, arithmetic and copies ran while one was open for 3% -> 0% of each run, Pallas kernels for 0% -> 0%
where the time goes in v1:
time: 63.3 us; the launch traced here: 63 us
  Pallas kernels  56.4 us (89%)
  local copies, waits for them, and re-layouts  4.73 us (7%)
  other arithmetic  1.14 us (2%)
  between operations  0.72 us (1%)
    pallas_call x1, Pallas kernels, shards(): pl.pallas_call(functools.partial(scan_kernel, sizes), out_shape=[jax.Shap...  49.6 us
    pallas_call x1, Pallas kernels, shards(): pl.pallas_call(functools.partial(block_kernel, scale, at_once), grid=(hea...  6.81 us
    unnamed x16, local copies, waits for them, and re-layouts  4.73 us

profile of v1, /device:TPU:1, one launch (start us, length us, event | category | flops | bytes accessed | tf_op | source)
XLA Modules:
  0.0 63.0 jit_solution(11971742348274242706)
XLA Ops:
  0.6 0.0 copy-start
  0.6 0.7 %convert_element_type.10 = f32[128]{0:T(128)S(1)} convert(s32[128]{0:T(128)} %param.9) | non-fusion elementwise | flops 128 | bytes 1024 | tf_op jit(solution)/shard_map/convert_element_type | solution.py:241
  1.4 0.3 fusion
  1.7 0.1 pad_maximum_fusion
  1.8 0.0 copy-start.4
  1.8 0.0 copy-start.5
  1.8 0.0 copy-done
  1.8 0.0 copy-start.1
  1.8 1.1 %copy-done.1 = bf16[128,2048]{1,0:T(8,128)(2,1)S(1)} copy-done((bf16[128,2048]{1,0:T(8,128)(2,1)S(1)}, bf16[128,2048]{1,0:T(8,128)(2,1)}, u32[]{:S(2)}) %copy-start.1) | copy-done | bytes 524312
  2.9 0.0 copy-start.2
  2.9 1.0 %copy-done.2 = bf16[128,2048]{1,0:T(8,128)(2,1)S(1)} copy-done((bf16[128,2048]{1,0:T(8,128)(2,1)S(1)}, bf16[128,2048]{1,0:T(8,128)(2,1)}, u32[]{:S(2)}) %copy-start.2) | copy-done | bytes 524312
  3.9 0.0 copy-start.3
  3.9 1.0 %copy-done.3 = bf16[128,2048]{1,0:T(8,128)(2,1)S(1)} copy-done((bf16[128,2048]{1,0:T(8,128)(2,1)S(1)}, bf16[128,2048]{1,0:T(8,128)(2,1)}, u32[]{:S(2)}) %copy-start.3) | copy-done | bytes 524312
  5.0 49.6 %scan.1 = (bf16[16,128,128]{2,1,0:T(8,128)(2,1)S(1)}, bf16[16,128,128]{2,1,0:T(8,128)(2,1)S(1)}) custom-call(bf16[128,2048]{1,0:T(8,128)(2,1)S(1)} %copy-done, bf16[128,2048]{1,0:T(8,128)(2,1)S(1)} %copy-done.1, bf16[128,2048]{1,0:T(8,128)(2,1)S(1)} %copy-done.2, bf16[128,2048]{1,0:T(8,128)(2,1)S(1)} %copy-done.3, f32[128,128]{1,0:T(8,128)S(1)} %get-tuple-element.11.cos_ref, ...), custom_call_target="tpu_custom_call" | custom-call | tf_op jit(solution)/shard_map/scan/pallas_call | solution.py:254
  54.5 0.0 copy-done.4
  54.6 0.0 copy-done.5
  54.6 0.0 copy-start.6
  54.6 0.8 %copy-done.6 = bf16[16,128,128]{2,1,0:T(8,128)(2,1)} copy-done((bf16[16,128,128]{2,1,0:T(8,128)(2,1)}, bf16[16,128,128]{2,1,0:T(8,128)(2,1)S(1)}, u32[]{:S(2)}) %copy-start.6) | copy-done | bytes 524312
  55.4 0.0 copy-start.7
  55.4 0.8 %copy-done.7 = bf16[16,128,128]{2,1,0:T(8,128)(2,1)} copy-done((bf16[16,128,128]{2,1,0:T(8,128)(2,1)}, bf16[16,128,128]{2,1,0:T(8,128)(2,1)S(1)}, u32[]{:S(2)}) %copy-start.7) | copy-done | bytes 524312
  56.1 6.8 %block.1 = (bf16[128,2048]{1,0:T(8,128)(2,1)}, bf16[128,2048]{1,0:T(8,128)(2,1)}, bf16[128,2048]{1,0:T(8,128)(2,1)}, bf16[128,2048]{1,0:T(8,128)(2,1)}) custom-call(bf16[128,2048]{1,0:T(8,128)(2,1)} %q_ref.3, bf16[128,2048]{1,0:T(8,128)(2,1)} %k_ref.3, bf16[128,2048]{1,0:T(8,128)(2,1)} %v_ref.3, bf16[128,2048]{1,0:T(8,128)(2,1)} %g_ref.3, ...), custom_call_target="tpu_custom_call" | custom-call | tf_op jit(solution)/shard_map/block/pallas_call | solution.py:279
  (1 shorter events, 0.0 us)
Async XLA Ops:
  0.6 1.2 %copy-start = (bf16[128,2048]{1,0:T(8,128)(2,1)S(1)}, bf16[128,2048]{1,0:T(8,128)(2,1)}, u32[]{:S(2)}) copy-start(bf16[128,2048]{1,0:T(8,128)(2,1)} %q_ref.3) | copy-start | bytes 1572868
  1.8 52.8 %copy-start.4 = (f32[128,128]{1,0:T(8,128)}, f32[128,128]{1,0:T(8,128)S(1)}, u32[]{:S(2)}) copy-start(f32[128,128]{1,0:T(8,128)S(1)} %get-tuple-element.11.cos_ref) | copy-start | bytes 196612
  1.8 52.8 %copy-start.5 = (f32[128,128]{1,0:T(8,128)}, f32[128,128]{1,0:T(8,128)S(1)}, u32[]{:S(2)}) copy-start(f32[128,128]{1,0:T(8,128)S(1)} %get-tuple-element.12.sin_ref) | copy-start | bytes 196612
  1.8 1.1 %copy-start.1 = (bf16[128,2048]{1,0:T(8,128)(2,1)S(1)}, bf16[128,2048]{1,0:T(8,128)(2,1)}, u32[]{:S(2)}) copy-start(bf16[128,2048]{1,0:T(8,128)(2,1)} %k_ref.3) | copy-start | bytes 1572868
  2.9 1.0 %copy-start.2 = (bf16[128,2048]{1,0:T(8,128)(2,1)S(1)}, bf16[128,2048]{1,0:T(8,128)(2,1)}, u32[]{:S(2)}) copy-start(bf16[128,2048]{1,0:T(8,128)(2,1)} %v_ref.3) | copy-start | bytes 1572868
  3.9 1.0 %copy-start.3 = (bf16[128,2048]{1,0:T(8,128)(2,1)S(1)}, bf16[128,2048]{1,0:T(8,128)(2,1)}, u32[]{:S(2)}) copy-start(bf16[128,2048]{1,0:T(8,128)(2,1)} %g_ref.3) | copy-start | bytes 1572868
  54.6 0.8 %copy-start.6 = (bf16[16,128,128]{2,1,0:T(8,128)(2,1)}, bf16[16,128,128]{2,1,0:T(8,128)(2,1)S(1)}, u32[]{:S(2)}) copy-start(bf16[16,128,128]{2,1,0:T(8,128)(2,1)S(1)} %get-tuple-element.6.before_ref) | copy-start | bytes 1572868
  55.4 0.8 %copy-start.7 = (bf16[16,128,128]{2,1,0:T(8,128)(2,1)}, bf16[16,128,128]{2,1,0:T(8,128)(2,1)S(1)}, u32[]{:S(2)}) copy-start(bf16[16,128,128]{2,1,0:T(8,128)(2,1)S(1)} %get-tuple-element.7.after_ref) | copy-start | bytes 1572868

commit v2 on v1

v2 whole, which is shorter than its diff:
```python
import functools
import math

import jax
import jax.numpy as jnp
from jax import lax
from jax.experimental import pallas as pl
from jax.experimental.pallas import tpu as pltpu
from jax.sharding import PartitionSpec as P

D_HEAD = 128
CORES = 2
HALVES = 2
F32, BF16 = (jnp.float32, jnp.bfloat16)


def rotate(rows, cosine, sine):
    rows = rows.astype(F32)
    return rows * cosine + pltpu.roll(rows, D_HEAD // 2, 1) * sine


def unrotate(rows, cosine, sine):
    return rows * cosine - pltpu.roll(rows, D_HEAD // 2, 1) * sine


def dot(left, right, left_dim, right_dim):
    return lax.dot_general(
        left, right, (((left_dim,), (right_dim,)), ((), ())), preferred_element_type=F32
    )


def columns(head, width=D_HEAD):
    return pl.ds(pl.multiple_of(head * width, width), width)


def scan_kernel(
    sizes, scale,
    q_hbm, k_hbm, v_hbm, g_hbm, pos_hbm,
    attended_ref, query_grad_ref, key_grad_ref, value_grad_ref,
    q_ref, k_ref, v_ref, g_ref, pos_ref, cos_ref, sin_ref, qrot, krot, partial, before, after,
    theirs, own, pin, chip, xin, row, yin, plane, zin, yout, ybase, xout, xbase, pout, pbase,
    in_s, pos_s, core_s, core_r, x_s, x_r, y_s, y_r, z_s, z_r, yb_s, yb_r, xb_s, xb_r, cb_s, cb_r,
):
    nx, ny, nz, per = sizes
    inner, outer = (lax.axis_index("inner"), lax.axis_index("outer"))
    x, c = (inner // CORES, lax.rem(inner, CORES))
    z, y = (outer // ny, lax.rem(outer, ny))
    tall = D_HEAD // HALVES
    part = tall // ny
    other = 1 - c
    tokens = q_ref.shape[0]

    def at(xx, cc, yy, zz):
        return {"inner": xx * CORES + cc, "outer": zz * ny + yy}

    def shifted(place, by, count):
        return lax.rem(place + by, count)

    partner = at(x, other, y, z)
    x_dev = [at(shifted(x, d, nx), c, y, z) for d in range(nx)]
    y_dev = [at(x, c, shifted(y, d, ny), z) for d in range(ny)]
    z_dev = [at(x, c, y, shifted(z, d, nz)) for d in range(nz)]
    barrier = pltpu.get_barrier_semaphore()
    peers = [partner] + x_dev[1:] + y_dev[1:] + z_dev[1:]
    for peer in peers:
        pl.semaphore_signal(barrier, inc=1, device_id=peer, device_id_type=pl.DeviceIdType.MESH)

    far_first = sorted(range(nx), key=lambda d: (d == 0, -min(d, nx - d)))
    near_first = far_first[::-1]
    arrays = ((k_hbm, k_ref), (v_hbm, v_ref), (q_hbm, q_ref), (g_hbm, g_ref))

    def fetch(side, d):
        cols = columns(shifted(x, d, nx) * CORES + (c if side else other), per * D_HEAD)
        return [
            pltpu.make_async_copy(src.at[:, cols], dst.at[:, cols], in_s.at[n, side, d])
            for n, (src, dst) in enumerate(arrays)
        ]

    place = pltpu.make_async_copy(pos_hbm, pos_ref, pos_s)
    place.start()
    for side in (0, 1):
        for d in far_first:
            for copy in fetch(side, d):
                copy.start()

    sent = []

    def remote(src, dst, send, recv, device):
        return pltpu.make_async_remote_copy(
            src_ref=src, dst_ref=dst, send_sem=send, recv_sem=recv,
            device_id=device, device_id_type=pl.DeviceIdType.MESH,
        )

    def post(*args):
        copy = remote(*args)
        copy.start()
        sent.append(copy)

    place.wait()
    half = D_HEAD // 2
    pair = lax.broadcasted_iota(jnp.int32, (half, tokens), 0).astype(F32)
    angle = pos_ref[...].astype(F32) * jnp.exp(pair * (-2.0 * math.log(500000.0) / D_HEAD))
    cosine, sine = (jnp.cos(angle), jnp.sin(angle))
    cos_ref[...] = jnp.concatenate([cosine, cosine], axis=0).T
    sin_ref[...] = jnp.concatenate([-sine, sine], axis=0).T

    def head_of(xx, cc, j):
        return (xx * CORES + cc) * per + j

    def states(head, put):
        cols = columns(head)
        cosine, sine = (cos_ref[...], sin_ref[...])
        key = rotate(k_ref[:, cols], cosine, sine).astype(BF16)
        krot[:, cols] = key
        put[0] = dot(key, v_ref[:, cols], 0, 0)
        query = rotate(q_ref[:, cols], cosine, sine).astype(BF16)
        qrot[:, cols] = query
        put[1] = dot(query, g_ref[:, cols], 0, 0)

    def in_block(head):
        cols = columns(head)
        query, key, value, grad = (qrot[:, cols], krot[:, cols], v_ref[:, cols], g_ref[:, cols])
        causal = lax.broadcasted_iota(jnp.int32, (tokens, tokens), 0) >= lax.broadcasted_iota(
            jnp.int32, (tokens, tokens), 1
        )
        scores = jnp.where(causal, dot(query, key, 1, 1), 0.0).astype(BF16)
        grad_scores = jnp.where(causal, dot(grad, value, 1, 1), 0.0).astype(BF16)
        partial[0, :, cols] = dot(scores, value, 1, 0)
        partial[1, :, cols] = dot(grad_scores, key, 1, 0)
        partial[2, :, cols] = dot(grad_scores, query, 0, 0)
        partial[3, :, cols] = dot(scores, grad, 0, 0)

    def finish(head):
        cols = columns(head)
        cosine, sine = (cos_ref[...], sin_ref[...])
        first, last = (before[head], after[head])
        attended = partial[0, :, cols] + dot(qrot[:, cols], first, 1, 0)
        attended_ref[:, cols] = (scale * attended).astype(BF16)
        query_grad = scale * (partial[1, :, cols] + dot(g_ref[:, cols], first, 1, 1))
        query_grad_ref[:, cols] = unrotate(query_grad, cosine, sine).astype(BF16)
        key_grad = scale * (partial[2, :, cols] + dot(v_ref[:, cols], last, 1, 1))
        key_grad_ref[:, cols] = unrotate(key_grad, cosine, sine).astype(BF16)
        value_grad = scale * (partial[3, :, cols] + dot(krot[:, cols], last, 1, 0))
        value_grad_ref[:, cols] = value_grad.astype(BF16)

    def spans(n):
        return n // HALVES, pl.ds((n % HALVES) * tall, tall)

    def start_states(j):
        for d in far_first:
            xx = shifted(x, d, nx)
            if j == 0:
                for copy in fetch(0, d):
                    copy.wait()
            states(head_of(xx, other, j), theirs.at[xx, j])
            if j == 0 and d == far_first[0]:
                pl.semaphore_wait(barrier, len(peers))
            post(theirs.at[xx, j], pin.at[xx, j], core_s.at[d, j], core_r.at[d, j], partner)
        for d in far_first:
            xx = shifted(x, d, nx)
            if j == 0:
                for copy in fetch(1, d):
                    copy.wait()
            states(head_of(xx, c, j), own.at[xx, j])

    def send_x(j):
        for d in far_first:
            xx = shifted(x, d, nx)
            remote(theirs.at[xx, j], pin.at[xx, j], core_s.at[d, j], core_r.at[d, j], partner).wait_recv()
            if d:
                chip[xx, j] = own[xx, j] + pin[xx, j]
            else:
                xin[x, j] = own[x, j] + pin[x, j]
        for n in range(j * HALVES, (j + 1) * HALVES):
            rows = spans(n)[1]
            for d in far_first[:-1]:
                xx = shifted(x, d, nx)
                post(chip.at[xx, j, :, rows], xin.at[x, j, :, rows], x_s.at[d, n], x_r.at[d, n], x_dev[d])

    def got_x(n):
        j, rows = spans(n)
        for d in range(1, nx):
            src = shifted(x, nx - d, nx)
            remote(chip.at[src, j, :, rows], xin.at[src, j, :, rows], x_s.at[d, n], x_r.at[d, n], x_dev[d]).wait_recv()
        total = xin[0, j, :, rows]
        for xx in range(1, nx):
            total = total + xin[xx, j, :, rows]
        row[n] = total
        for d in range(1, ny):
            cut = pl.ds(pl.multiple_of(shifted(y, d, ny) * part, part), part)
            post(row.at[n, :, cut], yin.at[y, n], y_s.at[d, n], y_r.at[d, n], y_dev[d])
        yin[y, n] = row[n, :, pl.ds(pl.multiple_of(y * part, part), part)]

    def got_y(n):
        for d in range(1, ny):
            src = shifted(y, ny - d, ny)
            remote(yout.at[src, n], yin.at[src, n], y_s.at[d, n], y_r.at[d, n], y_dev[d]).wait_recv()
        total = yin[0, n]
        for yy in range(1, ny):
            total = total + yin[yy, n]
        plane[n] = total
        for d in sorted(range(1, nz), key=lambda d: -min(d, nz - d)):
            which = jnp.where(z + d >= nz, 1, 0)
            post(plane.at[n, which], zin.at[z, n], z_s.at[d, n], z_r.at[d, n], z_dev[d])
        zin[z, n] = jnp.zeros((part, D_HEAD), F32)

    def got_z(n):
        for d in range(1, nz):
            src = shifted(z, nz - d, nz)
            remote(plane.at[n, 0], zin.at[src, n], z_s.at[d, n], z_r.at[d, n], z_dev[d]).wait_recv()
        earlier = jnp.zeros((part, D_HEAD), F32)
        later = jnp.zeros((part, D_HEAD), F32)
        for zz in range(nz):
            piece = zin[zz, n]
            earlier = earlier + jnp.where(zz < z, piece, 0.0)
            later = later + jnp.where(zz > z, piece, 0.0)
        for yy in range(ny):
            yout[yy, n, 0] = earlier
            earlier = earlier + yin[yy, n, 0]
        for yy in reversed(range(ny)):
            yout[yy, n, 1] = later
            later = later + yin[yy, n, 1]
        mine = pl.ds(pl.multiple_of(y * part, part), part)
        for d in range(1, ny):
            yy = shifted(y, d, ny)
            post(yout.at[yy, n], ybase.at[n, :, mine], yb_s.at[d, n], yb_r.at[d, n], y_dev[d])
        ybase[n, :, mine] = yout[y, n]

    def got_yb(n):
        j, rows = spans(n)
        for d in range(1, ny):
            src = shifted(y, ny - d, ny)
            cut = pl.ds(pl.multiple_of(src * part, part), part)
            remote(yout.at[src, n], ybase.at[n, :, cut], yb_s.at[d, n], yb_r.at[d, n], y_dev[d]).wait_recv()
        earlier = ybase[n, 0]
        for xx in range(nx):
            xout[xx, n, 0] = earlier
            earlier = earlier + xin[xx, j, 0, rows]
        later = ybase[n, 1]
        for xx in reversed(range(nx)):
            xout[xx, n, 1] = later
            later = later + xin[xx, j, 1, rows]
        for d in far_first[:-1]:
            xx = shifted(x, d, nx)
            post(xout.at[xx, n], xbase.at[x, n], xb_s.at[d, n], xb_r.at[d, n], x_dev[d])
        xbase[x, n] = xout[x, n]

    def got_xb(n):
        j, rows = spans(n)
        for d in near_first:
            src = shifted(x, nx - d, nx)
            if d:
                remote(xout.at[src, n], xbase.at[src, n], xb_s.at[d, n], xb_r.at[d, n], x_dev[d]).wait_recv()
            keys, queries = (xbase[src, n, 0], xbase[src, n, 1])
            pout[src, n, 0] = keys + jnp.where(c == 0, own[src, j, 0, rows], 0.0)
            pout[src, n, 1] = queries + jnp.where(c == 1, own[src, j, 1, rows], 0.0)
            post(pout.at[src, n], pbase.at[src, n], cb_s.at[d, n], cb_r.at[d, n], partner)
            head = head_of(src, c, j)
            before[head, rows] = (keys + jnp.where(c == 1, pin[src, j, 0, rows], 0.0)).astype(BF16)
            after[head, rows] = (queries + jnp.where(c == 0, pin[src, j, 1, rows], 0.0)).astype(BF16)

    def got_cb(n):
        j, rows = spans(n)
        for d in near_first:
            src = shifted(x, nx - d, nx)
            remote(pout.at[src, n], pbase.at[src, n], cb_s.at[d, n], cb_r.at[d, n], partner).wait_recv()
            head = head_of(src, other, j)
            before[head, rows] = pbase[src, n, 0].astype(BF16)
            after[head, rows] = pbase[src, n, 1].astype(BF16)

    def finish_side(j, cc):
        for d in near_first:
            finish(head_of(shifted(x, nx - d, nx), cc, j))

    heads = iter(range(nx * CORES * per))

    def some_heads(count):
        for _ in range(count):
            head = next(heads, None)
            if head is not None:
                in_block(head)

    chunks = per * HALVES
    for j in range(per):
        start_states(j)
        send_x(j)
    some_heads(5)
    stages = ((got_x, 0.0), (got_y, 3.1), (got_z, 8.4), (got_yb, 11.5), (got_xb, 16.7))
    events = sorted(
        (lag + 2.8 * 4 / chunks * n, k, n) for k, (_, lag) in enumerate(stages) for n in range(chunks)
    )
    for _, k, n in events:
        stages[k][0](n)
        if k < 2:
            some_heads(2)
        if k == 3 and n == chunks - 1:
            some_heads(nx * CORES * per)
            for j in range(per - 1):
                for m in range(j * HALVES, (j + 1) * HALVES):
                    got_cb(m)
                finish_side(j, c)
                finish_side(j, other)
    finish_side(per - 1, c)
    for n in range((per - 1) * HALVES, chunks):
        got_cb(n)
    finish_side(per - 1, other)
    for copy in sent:
        copy.wait_send()


def write_kernel(*refs):
    count = len(refs) // 2
    sem = refs[-1]
    copies = [pltpu.make_async_copy(refs[n], refs[count + n], sem.at[n]) for n in range(count)]
    for copy in copies:
        copy.start()
    for copy in copies:
        copy.wait()


def shards(sizes, queries, keys, values, out_grad, positions):
    nx, ny, nz, per = sizes
    tokens, width = queries.shape
    heads = width // D_HEAD
    total_tokens = tokens * lax.axis_size("inner") * lax.axis_size("outer")
    scale = (D_HEAD * total_tokens) ** (-0.5)
    chunks = per * HALVES
    tall = D_HEAD // HALVES
    part = tall // ny

    tokens_bf16 = pltpu.VMEM((tokens, width), BF16)
    table = pltpu.VMEM((tokens, D_HEAD), F32)
    state = pltpu.VMEM((heads, D_HEAD, D_HEAD), BF16)
    by_x = pltpu.VMEM((nx, per, 2, D_HEAD, D_HEAD), F32)
    by_x_chunk = pltpu.VMEM((nx, chunks, 2, tall, D_HEAD), F32)
    by_y = pltpu.VMEM((ny, chunks, 2, part, D_HEAD), F32)
    mine = pltpu.VMEM((chunks, 2, tall, D_HEAD), F32)
    in_vmem = pl.BlockSpec(memory_space=pltpu.VMEM)
    in_hbm = pl.BlockSpec(memory_space=pltpu.HBM)
    sems = [pltpu.SemaphoreType.DMA((4, 2, nx)), pltpu.SemaphoreType.DMA]
    for count in ((nx, per), (nx, chunks), (ny, chunks), (nz, chunks), (ny, chunks), (nx, chunks), (nx, chunks)):
        sems += [pltpu.SemaphoreType.DMA(count)] * 2
    results = [jax.ShapeDtypeStruct((tokens, width), BF16)] * 4
    arrays = (queries, keys, values, out_grad, positions.reshape(1, tokens))
    arrays = [pltpu.with_memory_space_constraint(a, pltpu.HBM) for a in arrays]
    outputs = pl.pallas_call(
        functools.partial(scan_kernel, sizes, scale),
        out_shape=[pltpu.VMEM((tokens, width), BF16)] * 4,
        in_specs=[in_hbm] * 5,
        out_specs=[in_vmem] * 4,
        scratch_shapes=[tokens_bf16] * 4 + [pltpu.VMEM((1, tokens), jnp.int32)] + [table] * 2 + [tokens_bf16] * 2
        + [pltpu.VMEM((4, tokens, width), F32), state, state]
        + [by_x] * 5 + [mine, by_y]
        + [pltpu.VMEM((chunks, 2, part, D_HEAD), F32), pltpu.VMEM((nz, chunks, part, D_HEAD), F32)]
        + [by_y, mine] + [by_x_chunk] * 4 + sems,
        compiler_params=pltpu.CompilerParams(
            collective_id=0, has_side_effects=True, vmem_limit_bytes=48 * 1024 * 1024
        ),
        name="scan",
    )(*arrays)
    return pl.pallas_call(
        write_kernel,
        out_shape=results,
        in_specs=[in_vmem] * 4,
        out_specs=[in_hbm] * 4,
        scratch_shapes=[pltpu.SemaphoreType.DMA((4,))],
        name="write",
    )(*[pltpu.with_memory_space_constraint(a, pltpu.VMEM) for a in outputs])


def solution(mesh):
    inner, outer = (mesh.shape["inner"], mesh.shape["outer"])
    ny = 4 if outer % 16 == 0 else 2
    sizes = (inner // CORES, ny, outer // ny, 16 // inner)
    both = P(("outer", "inner"), None)
    return jax.shard_map(
        functools.partial(shards, sizes),
        mesh=mesh,
        in_specs=(both,) * 4 + (P(("outer", "inner")),),
        out_specs=(both,) * 4,
        check_vma=False,
    )
```

time: 63.3 us -> 50.6 us (0.80)
  Pallas kernels: 56.4 us -> 49.8 us
  local copies, waits for them, and re-layouts: 4.73 us -> 0 us
  other arithmetic: 1.14 us -> 0 us
    pallas_call x2, Pallas kernels: 56.4 us -> 49.8 us  [the longest x1 48.5 us: shards(): pl.pallas_call(functools.partial(scan_kernel, sizes, scale), out_shape=[p...]
    unnamed x16 -> x0, local copies, waits for them, and re-layouts: 4.73 us -> none
    convert_element_type x1 -> x0, other arithmetic: 0.72 us -> none  [shards(): angle = positions.astype(F32)[:, None] * jnp.exp(spacing)[None, :]]
where the time goes in v2:
time: 50.6 us; the launch traced here: 50.5 us
  Pallas kernels  49.8 us (98%)
  between operations  0.64 us (1%)
    pallas_call x1, Pallas kernels, shards(): pl.pallas_call(functools.partial(scan_kernel, sizes, scale), out_shape=[p...  48.5 us
    pallas_call x1, Pallas kernels, shards(): pl.pallas_call(write_kernel, out_shape=results, in_specs=[in_vmem] * 4, o...  1.35 us

profile of v2, /device:TPU:1, one launch (start us, length us, event | category | flops | bytes accessed | tf_op | source)
XLA Modules:
  0.0 50.5 jit_solution(13145654370930784852)
XLA Ops:
  0.6 48.5 %scan.1 = (bf16[128,2048]{1,0:T(8,128)(2,1)S(1)}, bf16[128,2048]{1,0:T(8,128)(2,1)S(1)}, bf16[128,2048]{1,0:T(8,128)(2,1)S(1)}, bf16[128,2048]{1,0:T(8,128)(2,1)S(1)}) custom-call(bf16[128,2048]{1,0:T(8,128)(2,1)} %q_hbm.1, bf16[128,2048]{1,0:T(8,128)(2,1)} %k_hbm.1, bf16[128,2048]{1,0:T(8,128)(2,1)} %v_hbm.1, bf16[128,2048]{1,0:T(8,128)(2,1)} %g_hbm.1, ...), custom_call_target="tpu_custom_call" | custom-call | tf_op jit(solution)/shard_map/scan/pallas_call | solution.py:346
  49.1 1.3 %write.1 = (bf16[128,2048]{1,0:T(8,128)(2,1)}, bf16[128,2048]{1,0:T(8,128)(2,1)}, bf16[128,2048]{1,0:T(8,128)(2,1)}, bf16[128,2048]{1,0:T(8,128)(2,1)}) custom-call(bf16[128,2048]{1,0:T(8,128)(2,1)S(1)} %get-tuple-element.8.refs_0_, bf16[128,2048]{1,0:T(8,128)(2,1)S(1)} %get-tuple-element.9.refs_1_, bf16[128,2048]{1,0:T(8,128)(2,1)S(1)} %get-tuple-element.10.refs_2_, ...), custom_call_target="tpu_custom_call" | custom-call | tf_op jit(solution)/shard_map/write/pallas_call | solution.py:361

commit v3 on v2

--- a/solution.py
+++ b/solution.py
@@ -39,12 +39,12 @@
     attended_ref, query_grad_ref, key_grad_ref, value_grad_ref,
     q_ref, k_ref, v_ref, g_ref, pos_ref, cos_ref, sin_ref, qrot, krot, partial, before, after,
     theirs, own, pin, chip, xin, row, yin, plane, zin, yout, ybase, xout, xbase, pout, pbase,
-    in_s, pos_s, core_s, core_r, x_s, x_r, y_s, y_r, z_s, z_r, yb_s, yb_r, xb_s, xb_r, cb_s, cb_r,
+    in_s, core_s, core_r, x_s, x_r, y_s, y_r, z_s, z_r, yb_s, yb_r, xb_s, xb_r, cb_s, cb_r,
 ):
     nx, ny, nz, per = sizes
     inner, outer = (lax.axis_index("inner"), lax.axis_index("outer"))
-    x, c = (inner // CORES, lax.rem(inner, CORES))
-    z, y = (outer // ny, lax.rem(outer, ny))
+    x, z = (lax.div(inner, CORES), lax.div(outer, ny))
+    c, y = (inner - x * CORES, outer - z * ny)
     tall = D_HEAD // HALVES
     part = tall // ny
     other = 1 - c
@@ -54,12 +54,16 @@
         return {"inner": xx * CORES + cc, "outer": zz * ny + yy}
 
     def shifted(place, by, count):
-        return lax.rem(place + by, count)
+        return place + by - jnp.where(place + by >= count, count, 0) if by else place
 
     partner = at(x, other, y, z)
     x_dev = [at(shifted(x, d, nx), c, y, z) for d in range(nx)]
     y_dev = [at(x, c, shifted(y, d, ny), z) for d in range(ny)]
     z_dev = [at(x, c, y, shifted(z, d, nz)) for d in range(nz)]
+    arrays = ((pos_hbm, pos_ref), (k_hbm, k_ref), (v_hbm, v_ref), (q_hbm, q_ref), (g_hbm, g_ref))
+    fetched = [pltpu.make_async_copy(src, dst, in_s.at[n]) for n, (src, dst) in enumerate(arrays)]
+    for copy in fetched:
+        copy.start()
     barrier = pltpu.get_barrier_semaphore()
     peers = [partner] + x_dev[1:] + y_dev[1:] + z_dev[1:]
     for peer in peers:
@@ -67,22 +71,6 @@
 
     far_first = sorted(range(nx), key=lambda d: (d == 0, -min(d, nx - d)))
     near_first = far_first[::-1]
-    arrays = ((k_hbm, k_ref), (v_hbm, v_ref), (q_hbm, q_ref), (g_hbm, g_ref))
-
-    def fetch(side, d):
-        cols = columns(shifted(x, d, nx) * CORES + (c if side else other), per * D_HEAD)
-        return [
-            pltpu.make_async_copy(src.at[:, cols], dst.at[:, cols], in_s.at[n, side, d])
-            for n, (src, dst) in enumerate(arrays)
-        ]
-
-    place = pltpu.make_async_copy(pos_hbm, pos_ref, pos_s)
-    place.start()
-    for side in (0, 1):
-        for d in far_first:
-            for copy in fetch(side, d):
-                copy.start()
-
     sent = []
 
     def remote(src, dst, send, recv, device):
@@ -96,7 +84,7 @@
         copy.start()
         sent.append(copy)
 
-    place.wait()
+    fetched[0].wait()
     half = D_HEAD // 2
     pair = lax.broadcasted_iota(jnp.int32, (half, tokens), 0).astype(F32)
     angle = pos_ref[...].astype(F32) * jnp.exp(pair * (-2.0 * math.log(500000.0) / D_HEAD))
@@ -146,50 +134,40 @@
     def spans(n):
         return n // HALVES, pl.ds((n % HALVES) * tall, tall)
 
-    def start_states(j):
-        for d in far_first:
-            xx = shifted(x, d, nx)
-            if j == 0:
-                for copy in fetch(0, d):
-                    copy.wait()
-            states(head_of(xx, other, j), theirs.at[xx, j])
-            if j == 0 and d == far_first[0]:
-                pl.semaphore_wait(barrier, len(peers))
-            post(theirs.at[xx, j], pin.at[xx, j], core_s.at[d, j], core_r.at[d, j], partner)
-        for d in far_first:
-            xx = shifted(x, d, nx)
-            if j == 0:
-                for copy in fetch(1, d):
-                    copy.wait()
-            states(head_of(xx, c, j), own.at[xx, j])
-
-    def send_x(j):
-        for d in far_first:
-            xx = shifted(x, d, nx)
+    def send_core(d, j):
+        xx = shifted(x, d, nx)
+        states(head_of(xx, other, j), theirs.at[xx, j])
+        if j == 0 and d == far_first[0]:
+            pl.semaphore_wait(barrier, len(peers))
+        post(theirs.at[xx, j], pin.at[xx, j], core_s.at[d, j], core_r.at[d, j], partner)
+
+    def keep_own(d, j):
+        xx = shifted(x, d, nx)
+        states(head_of(xx, c, j), own.at[xx, j])
+
+    def send_x(d, n):
+        j, rows = spans(n)
+        xx = shifted(x, d, nx)
+        if n % HALVES == 0:
             remote(theirs.at[xx, j], pin.at[xx, j], core_s.at[d, j], core_r.at[d, j], partner).wait_recv()
-            if d:
-                chip[xx, j] = own[xx, j] + pin[xx, j]
-            else:
-                xin[x, j] = own[x, j] + pin[x, j]
-        for n in range(j * HALVES, (j + 1) * HALVES):
-            rows = spans(n)[1]
-            for d in far_first[:-1]:
-                xx = shifted(x, d, nx)
-                post(chip.at[xx, j, :, rows], xin.at[x, j, :, rows], x_s.at[d, n], x_r.at[d, n], x_dev[d])
+        if d:
+            chip[xx, n] = own[xx, j, :, rows] + pin[xx, j, :, rows]
+            post(chip.at[xx, n], xin.at[x, n], x_s.at[d, n], x_r.at[d, n], x_dev[d])
+        else:
+            xin[x, n] = own[x, j, :, rows] + pin[x, j, :, rows]
 
     def got_x(n):
-        j, rows = spans(n)
         for d in range(1, nx):
             src = shifted(x, nx - d, nx)
-            remote(chip.at[src, j, :, rows], xin.at[src, j, :, rows], x_s.at[d, n], x_r.at[d, n], x_dev[d]).wait_recv()
-        total = xin[0, j, :, rows]
+            remote(chip.at[src, n], xin.at[src, n], x_s.at[d, n], x_r.at[d, n], x_dev[d]).wait_recv()
+        total = xin[0, n]
         for xx in range(1, nx):
-            total = total + xin[xx, j, :, rows]
-        row[n] = total
-        for d in range(1, ny):
-            cut = pl.ds(pl.multiple_of(shifted(y, d, ny) * part, part), part)
-            post(row.at[n, :, cut], yin.at[y, n], y_s.at[d, n], y_r.at[d, n], y_dev[d])
-        yin[y, n] = row[n, :, pl.ds(pl.multiple_of(y * part, part), part)]
+            total = total + xin[xx, n]
+        for yy in range(ny):
+            row[n, yy] = total[:, yy * part : (yy + 1) * part]
+        for d in sorted(range(1, ny), key=lambda d: -min(d, ny - d)):
+            post(row.at[n, shifted(y, d, ny)], yin.at[y, n], y_s.at[d, n], y_r.at[d, n], y_dev[d])
+        yin[y, n] = row[n, y]
 
     def got_y(n):
         for d in range(1, ny):
@@ -220,26 +198,24 @@
         for yy in reversed(range(ny)):
             yout[yy, n, 1] = later
             later = later + yin[yy, n, 1]
-        mine = pl.ds(pl.multiple_of(y * part, part), part)
-        for d in range(1, ny):
-            yy = shifted(y, d, ny)
-            post(yout.at[yy, n], ybase.at[n, :, mine], yb_s.at[d, n], yb_r.at[d, n], y_dev[d])
-        ybase[n, :, mine] = yout[y, n]
+        for d in sorted(range(1, ny), key=lambda d: -min(d, ny - d)):
+            post(yout.at[shifted(y, d, ny), n], ybase.at[n, y], yb_s.at[d, n], yb_r.at[d, n], y_dev[d])
+        ybase[n, y] = yout[y, n]
 
     def got_yb(n):
-        j, rows = spans(n)
         for d in range(1, ny):
             src = shifted(y, ny - d, ny)
-            cut = pl.ds(pl.multiple_of(src * part, part), part)
-            remote(yout.at[src, n], ybase.at[n, :, cut], yb_s.at[d, n], yb_r.at[d, n], y_dev[d]).wait_recv()
-        earlier = ybase[n, 0]
-        for xx in range(nx):
-            xout[xx, n, 0] = earlier
-            earlier = earlier + xin[xx, j, 0, rows]
-        later = ybase[n, 1]
-        for xx in reversed(range(nx)):
-            xout[xx, n, 1] = later
-            later = later + xin[xx, j, 1, rows]
+            remote(yout.at[src, n], ybase.at[n, src], yb_s.at[d, n], yb_r.at[d, n], y_dev[d]).wait_recv()
+        for cut in range(ny):
+            rows = pl.ds(cut * part, part)
+            earlier = ybase[n, cut, 0]
+            for xx in range(nx):
+                xout[xx, n, 0, rows] = earlier
+                earlier = earlier + xin[xx, n, 0, rows]
+            later = ybase[n, cut, 1]
+            for xx in reversed(range(nx)):
+                xout[xx, n, 1, rows] = later
+                later = later + xin[xx, n, 1, rows]
         for d in far_first[:-1]:
             xx = shifted(x, d, nx)
             post(xout.at[xx, n], xbase.at[x, n], xb_s.at[d, n], xb_r.at[d, n], x_dev[d])
@@ -281,29 +257,32 @@
                 in_block(head)
 
     chunks = per * HALVES
+    for copy in fetched[1:]:
+        copy.wait()
     for j in range(per):
-        start_states(j)
-        send_x(j)
-    some_heads(5)
-    stages = ((got_x, 0.0), (got_y, 3.1), (got_z, 8.4), (got_yb, 11.5), (got_xb, 16.7))
+        for d in far_first:
+            send_core(d, j)
+        for d in far_first:
+            keep_own(d, j)
+        for n in range(j * HALVES, (j + 1) * HALVES):
+            for d in far_first:
+                send_x(d, n)
+    some_heads(16)
+    stages = ((got_x, 0.0), (got_y, 3.0), (got_z, 8.0), (got_yb, 11.3), (got_xb, 100))
     events = sorted(
-        (lag + 2.8 * 4 / chunks * n, k, n) for k, (_, lag) in enumerate(stages) for n in range(chunks)
+        (lag + 9.6 / chunks * n, k, n) for k, (_, lag) in enumerate(stages) for n in range(chunks)
     )
     for _, k, n in events:
         stages[k][0](n)
-        if k < 2:
-            some_heads(2)
-        if k == 3 and n == chunks - 1:
+        if k == 0:
+            some_heads(0)
+        if k == 4 and n % HALVES == HALVES - 1:
+            j = n // HALVES
             some_heads(nx * CORES * per)
-            for j in range(per - 1):
-                for m in range(j * HALVES, (j + 1) * HALVES):
-                    got_cb(m)
-                finish_side(j, c)
-                finish_side(j, other)
-    finish_side(per - 1, c)
-    for n in range((per - 1) * HALVES, chunks):
-        got_cb(n)
-    finish_side(per - 1, other)
+            finish_side(j, c)
+            for m in range(j * HALVES, n + 1):
+                got_cb(m)
+            finish_side(j, other)
     for copy in sent:
         copy.wait_send()
 
@@ -334,10 +313,10 @@
     by_x = pltpu.VMEM((nx, per, 2, D_HEAD, D_HEAD), F32)
     by_x_chunk = pltpu.VMEM((nx, chunks, 2, tall, D_HEAD), F32)
     by_y = pltpu.VMEM((ny, chunks, 2, part, D_HEAD), F32)
-    mine = pltpu.VMEM((chunks, 2, tall, D_HEAD), F32)
+    mine = pltpu.VMEM((chunks, ny, 2, part, D_HEAD), F32)
     in_vmem = pl.BlockSpec(memory_space=pltpu.VMEM)
     in_hbm = pl.BlockSpec(memory_space=pltpu.HBM)
-    sems = [pltpu.SemaphoreType.DMA((4, 2, nx)), pltpu.SemaphoreType.DMA]
+    sems = [pltpu.SemaphoreType.DMA((5,))]
     for count in ((nx, per), (nx, chunks), (ny, chunks), (nz, chunks), (ny, chunks), (nx, chunks), (nx, chunks)):
         sems += [pltpu.SemaphoreType.DMA(count)] * 2
     results = [jax.ShapeDtypeStruct((tokens, width), BF16)] * 4
@@ -350,7 +329,7 @@
         out_specs=[in_vmem] * 4,
         scratch_shapes=[tokens_bf16] * 4 + [pltpu.VMEM((1, tokens), jnp.int32)] + [table] * 2 + [tokens_bf16] * 2
         + [pltpu.VMEM((4, tokens, width), F32), state, state]
-        + [by_x] * 5 + [mine, by_y]
+        + [by_x] * 3 + [by_x_chunk] * 2 + [mine, by_y]
         + [pltpu.VMEM((chunks, 2, part, D_HEAD), F32), pltpu.VMEM((nz, chunks, part, D_HEAD), F32)]
         + [by_y, mine] + [by_x_chunk] * 4 + sems,
         compiler_params=pltpu.CompilerParams(

time: 50.6 us -> 49.2 us (0.972)
  Pallas kernels: 49.8 us -> 48.4 us
    pallas_call x1, Pallas kernels: 48.5 us -> 47.1 us  [shards(): pl.pallas_call(functools.partial(scan_kernel, sizes, scale), out_shape=[p...]
where the time goes in v3:
time: 49.2 us; the launch traced here: 49.1 us
  Pallas kernels  48.4 us (98%)
  between operations  0.64 us (1%)
    pallas_call x1, Pallas kernels, shards(): pl.pallas_call(functools.partial(scan_kernel, sizes, scale), out_shape=[p...  47.1 us
    pallas_call x1, Pallas kernels, shards(): pl.pallas_call(write_kernel, out_shape=results, in_specs=[in_vmem] * 4, o...  1.35 us

profile of v3, /device:TPU:1, one launch (start us, length us, event | category | flops | bytes accessed | tf_op | source)
XLA Modules:
  0.0 49.1 jit_solution(11787534634544156373)
XLA Ops:
  0.6 47.1 %scan.1 = (bf16[128,2048]{1,0:T(8,128)(2,1)S(1)}, bf16[128,2048]{1,0:T(8,128)(2,1)S(1)}, bf16[128,2048]{1,0:T(8,128)(2,1)S(1)}, bf16[128,2048]{1,0:T(8,128)(2,1)S(1)}) custom-call(bf16[128,2048]{1,0:T(8,128)(2,1)} %q_hbm.1, bf16[128,2048]{1,0:T(8,128)(2,1)} %k_hbm.1, bf16[128,2048]{1,0:T(8,128)(2,1)} %v_hbm.1, bf16[128,2048]{1,0:T(8,128)(2,1)} %g_hbm.1, ...), custom_call_target="tpu_custom_call" | custom-call | tf_op jit(solution)/shard_map/scan/pallas_call | solution.py:325
  47.7 1.3 %write.1 = (bf16[128,2048]{1,0:T(8,128)(2,1)}, bf16[128,2048]{1,0:T(8,128)(2,1)}, bf16[128,2048]{1,0:T(8,128)(2,1)}, bf16[128,2048]{1,0:T(8,128)(2,1)}) custom-call(bf16[128,2048]{1,0:T(8,128)(2,1)S(1)} %get-tuple-element.8.refs_0_, bf16[128,2048]{1,0:T(8,128)(2,1)S(1)} %get-tuple-element.9.refs_1_, bf16[128,2048]{1,0:T(8,128)(2,1)S(1)} %get-tuple-element.10.refs_2_, ...), custom_call_target="tpu_custom_call" | custom-call | tf_op jit(solution)/shard_map/write/pallas_call | solution.py:340

commit v4 on v3

--- a/solution.py
+++ b/solution.py
@@ -267,7 +267,7 @@
         for n in range(j * HALVES, (j + 1) * HALVES):
             for d in far_first:
                 send_x(d, n)
-    some_heads(16)
+    some_heads(6)
     stages = ((got_x, 0.0), (got_y, 3.0), (got_z, 8.0), (got_yb, 11.3), (got_xb, 100))
     events = sorted(
         (lag + 9.6 / chunks * n, k, n) for k, (_, lag) in enumerate(stages) for n in range(chunks)
@@ -275,11 +275,14 @@
     for _, k, n in events:
         stages[k][0](n)
         if k == 0:
-            some_heads(0)
+            some_heads(5)
         if k == 4 and n % HALVES == HALVES - 1:
             j = n // HALVES
             some_heads(nx * CORES * per)
             finish_side(j, c)
+            if n < chunks - 1:
+                while len(sent) > HALVES * (2 * nx - 1):
+                    sent.pop(0).wait_send()
             for m in range(j * HALVES, n + 1):
                 got_cb(m)
             finish_side(j, other)

time: 49.2 us -> 48.9 us (level)
  no operation moved by 1% of the time
where the time goes in v4:
time: 48.9 us; the launch traced here: 48.8 us
  Pallas kernels  48.2 us (99%)
  between operations  0.64 us (1%)
    pallas_call x1, Pallas kernels, shards(): pl.pallas_call(functools.partial(scan_kernel, sizes, scale), out_shape=[p...  46.8 us
    pallas_call x1, Pallas kernels, shards(): pl.pallas_call(write_kernel, out_shape=results, in_specs=[in_vmem] * 4, o...  1.35 us

profile of v4, /device:TPU:1, one launch (start us, length us, event | category | flops | bytes accessed | tf_op | source)
XLA Modules:
  0.0 48.8 jit_solution(17355055785355378864)
XLA Ops:
  0.6 46.8 %scan.1 = (bf16[128,2048]{1,0:T(8,128)(2,1)S(1)}, bf16[128,2048]{1,0:T(8,128)(2,1)S(1)}, bf16[128,2048]{1,0:T(8,128)(2,1)S(1)}, bf16[128,2048]{1,0:T(8,128)(2,1)S(1)}) custom-call(bf16[128,2048]{1,0:T(8,128)(2,1)} %q_hbm.1, bf16[128,2048]{1,0:T(8,128)(2,1)} %k_hbm.1, bf16[128,2048]{1,0:T(8,128)(2,1)} %v_hbm.1, bf16[128,2048]{1,0:T(8,128)(2,1)} %g_hbm.1, ...), custom_call_target="tpu_custom_call" | custom-call | tf_op jit(solution)/shard_map/scan/pallas_call | solution.py:328
  47.5 1.3 %write.1 = (bf16[128,2048]{1,0:T(8,128)(2,1)}, bf16[128,2048]{1,0:T(8,128)(2,1)}, bf16[128,2048]{1,0:T(8,128)(2,1)}, bf16[128,2048]{1,0:T(8,128)(2,1)}) custom-call(bf16[128,2048]{1,0:T(8,128)(2,1)S(1)} %get-tuple-element.8.refs_0_, bf16[128,2048]{1,0:T(8,128)(2,1)S(1)} %get-tuple-element.9.refs_1_, bf16[128,2048]{1,0:T(8,128)(2,1)S(1)} %get-tuple-element.10.refs_2_, ...), custom_call_target="tpu_custom_call" | custom-call | tf_op jit(solution)/shard_map/write/pallas_call | solution.py:343

commit v5 on v4

--- a/solution.py
+++ b/solution.py
@@ -268,12 +268,10 @@
             for d in far_first:
                 send_x(d, n)
     some_heads(6)
-    stages = ((got_x, 0.0), (got_y, 3.0), (got_z, 8.0), (got_yb, 11.3), (got_xb, 100))
-    events = sorted(
-        (lag + 9.6 / chunks * n, k, n) for k, (_, lag) in enumerate(stages) for n in range(chunks)
-    )
+    stages = (got_x, got_y, got_z, got_yb, got_xb)
+    events = [(0.0, 0, 0), (0.0, 0, 1), (0.0, 1, 0), (0.0, 0, 2), (0.0, 1, 1), (0.0, 0, 3), (0.0, 2, 0), (0.0, 1, 2), (0.0, 1, 3), (0.0, 3, 0), (0.0, 2, 1), (0.0, 2, 2), (0.0, 3, 1), (0.0, 2, 3), (0.0, 3, 2), (0.0, 3, 3), (0.0, 4, 0), (0.0, 4, 1), (0.0, 4, 2), (0.0, 4, 3)]
     for _, k, n in events:
-        stages[k][0](n)
+        stages[k](n)
         if k == 0:
             some_heads(5)
         if k == 4 and n % HALVES == HALVES - 1:

time: 48.9 us -> 48.6 us (level)
  no operation moved by 1% of the time
where the time goes in v5:
time: 48.6 us; the launch traced here: 48.5 us
  Pallas kernels  47.8 us (98%)
  between operations  0.64 us (1%)
    pallas_call x1, Pallas kernels, shards(): pl.pallas_call(functools.partial(scan_kernel, sizes, scale), out_shape=[p...  46.5 us
    pallas_call x1, Pallas kernels, shards(): pl.pallas_call(write_kernel, out_shape=results, in_specs=[in_vmem] * 4, o...  1.35 us

profile of v5, /device:TPU:1, one launch (start us, length us, event | category | flops | bytes accessed | tf_op | source)
XLA Modules:
  0.0 48.5 jit_solution(11082046162347331852)
XLA Ops:
  0.6 46.5 %scan.1 = (bf16[128,2048]{1,0:T(8,128)(2,1)S(1)}, bf16[128,2048]{1,0:T(8,128)(2,1)S(1)}, bf16[128,2048]{1,0:T(8,128)(2,1)S(1)}, bf16[128,2048]{1,0:T(8,128)(2,1)S(1)}) custom-call(bf16[128,2048]{1,0:T(8,128)(2,1)} %q_hbm.1, bf16[128,2048]{1,0:T(8,128)(2,1)} %k_hbm.1, bf16[128,2048]{1,0:T(8,128)(2,1)} %v_hbm.1, bf16[128,2048]{1,0:T(8,128)(2,1)} %g_hbm.1, ...), custom_call_target="tpu_custom_call" | custom-call | tf_op jit(solution)/shard_map/scan/pallas_call | solution.py:326
  47.1 1.3 %write.1 = (bf16[128,2048]{1,0:T(8,128)(2,1)}, bf16[128,2048]{1,0:T(8,128)(2,1)}, bf16[128,2048]{1,0:T(8,128)(2,1)}, bf16[128,2048]{1,0:T(8,128)(2,1)}) custom-call(bf16[128,2048]{1,0:T(8,128)(2,1)S(1)} %get-tuple-element.8.refs_0_, bf16[128,2048]{1,0:T(8,128)(2,1)S(1)} %get-tuple-element.9.refs_1_, bf16[128,2048]{1,0:T(8,128)(2,1)S(1)} %get-tuple-element.10.refs_2_, ...), custom_call_target="tpu_custom_call" | custom-call | tf_op jit(solution)/shard_map/write/pallas_call | solution.py:341
